TPU v7x, 256 devices: a whole 4x4x8 slice. The times are simulated.
256 devices in a mesh: lat: 16 (over z, x_lo), lon: 16 (over x_hi, y, core).
Axes of the slice: x: 4 (x_hi: 2, x_lo: 2; x = x_hi * 2 + x_lo), y: 4, z: 8, core: 2. Of those that a mesh axis runs over, the one named last changes fastest.
Arguments:
- tokens: bfloat16 [128, 256, 2, 1024], P('lat', 'lon'), may hold values from -6 to 6
- norm_gain: bfloat16 [1024], replicated, may hold values from 0.099609375 to 1.8984375
- q_weight: bfloat16 [1024, 1024], replicated, may hold values from -3 to 3
- k_weight: bfloat16 [1024, 1024], replicated, may hold values from -3 to 3
- v_weight: bfloat16 [1024, 1024], replicated, may hold values from -0.1875 to 0.1875
- o_weight: bfloat16 [1024, 1024], replicated, may hold values from -0.75 to 0.75
- band_start: int32 [16], replicated, may hold values from -15 to 0, as said below
- band_width: int32 [16], replicated, may hold values from 2 to 16, as said below
Outputs:
- mixed: bfloat16 [128, 256, 2, 1024], P('lat', 'lon')
Inputs may be any that keep to these rules, and one draw needn't show every extreme that they name: `band_width`: band 0 and band 16 - 1 have width 16; widths need not grow band by band. 1 - band_width[b] <= band_start[b], so a query's own block is always seen.
All inputs are finite; a program needn't handle non-finite values.
Results may differ from a plain program's by a relative error of at most 0.006.
Values may be sent and summed in bfloat16 or wider, within the bound.
No kernel may reach another device: no remote copies, remote signals or barrier semaphores. Data moves between devices by JAX's collectives and lax.ppermute only.
A program may use at most 128 MiB of HBM per device.

v0:
```python
import jax
import jax.numpy as jnp
from jax import lax
from jax.sharding import PartitionSpec as P

HD = 64


def with_halo(array, sides, width):
    for axis, dim in sides:
        devices, length = (lax.axis_size(axis), array.shape[dim])
        up = [(i, (i + 1) % devices) for i in range(devices - 1)]
        down = [(j, i) for i, j in up]
        last = lax.slice_in_dim(array, length - width, length, axis=dim)
        leading = lax.slice_in_dim(array, 0, width, axis=dim)
        before = lax.ppermute(last, axis, up)
        after = lax.ppermute(leading, axis, down)
        array = jnp.concatenate([before, array, after], axis=dim)
    return array


def from_behind(value, axis, steps):
    count = lax.axis_size(axis)
    pairs = [(source, (source + steps) % count) for source in range(count)]
    return lax.ppermute(value, axis, pairs)


def body(tokens, norm_gain, q_weight, k_weight, v_weight, o_weight, band_start, band_width):
    rows, columns, levels, width = tokens.shape
    heads = width // HD
    n_lon = lax.axis_size("lon")
    n_lat = lax.axis_size("lat")
    band = lax.axis_index("lat")
    block = lax.axis_index("lon")
    wide = tokens.astype(jnp.float32)
    normed = (
        wide
        * lax.rsqrt(jnp.mean(wide * wide, -1, keepdims=True) + 1e-06)
        * norm_gain.astype(jnp.float32)
    ).astype(jnp.bfloat16)
    flat = normed.reshape(-1, width)
    query = jnp.dot(flat, q_weight, preferred_element_type=jnp.float32).astype(jnp.bfloat16)
    keys = jnp.dot(flat, k_weight, preferred_element_type=jnp.float32).astype(jnp.bfloat16)
    values = jnp.dot(flat, v_weight, preferred_element_type=jnp.float32).astype(jnp.bfloat16)
    query_heads = query.reshape(-1, heads, HD)
    count_queries = query_heads.shape[0]
    pair = jnp.stack(
        [keys.reshape(rows, columns, levels, width), values.reshape(rows, columns, levels, width)]
    )
    padded = with_halo(pair, (("lat", 1),), 1)
    edges = jnp.stack([pair[:, 0], pair[:, rows - 1]], axis=1)
    across = from_behind(edges, "lon", n_lon // 2)
    top_row = across[:, 0]
    bottom_row = across[:, 1]
    first = jnp.where(band == 0, top_row, padded[:, 0])
    last = jnp.where(band == n_lat - 1, bottom_row, padded[:, rows + 1])
    extended = jnp.concatenate([first[:, None], padded[:, 1 : rows + 1], last[:, None]], axis=1)
    start_here = band_start[band]
    span_here = band_width[band]
    scale = HD ** (-0.5)

    def attend(state, piece, owner):
        inside = jnp.mod(owner - block - start_here, n_lon) < span_here

        def update(carry):
            top, total, weighted = carry
            key_heads = piece[0].reshape(-1, heads, HD)
            value_heads = piece[1].reshape(-1, heads, HD)
            scores = (
                jnp.einsum(
                    "qhd,khd->hqk", query_heads, key_heads, preferred_element_type=jnp.float32
                )
                * scale
            )
            new_top = jnp.maximum(top, jnp.max(scores, -1))
            raw = jnp.exp(scores - new_top[..., None])
            fade = jnp.exp(top - new_top)
            total = total * fade + jnp.sum(raw, -1)
            weighted = weighted * fade[..., None] + jnp.einsum(
                "hqk,khd->hqd",
                raw.astype(jnp.bfloat16),
                value_heads,
                preferred_element_type=jnp.float32,
            )
            return (new_top, total, weighted)

        def keep(carry):
            return carry

        return lax.cond(inside, update, keep, state)

    initial = (
        jnp.full((heads, count_queries), -1e30, jnp.float32),
        jnp.zeros((heads, count_queries), jnp.float32),
        jnp.zeros((heads, count_queries, HD), jnp.float32),
    )
    carry = initial
    piece = lax.all_gather(extended, "lon", axis=2, tiled=True)
    count = piece.shape[2] // columns
    split = jnp.moveaxis(piece.reshape(2, rows + 2, count, columns, levels, width), 2, 0)

    def advance(inner, element):
        single, offset = element
        return (attend(inner, single, offset), None)

    carry, unused = lax.scan(advance, carry, (split, jnp.arange(count, dtype=jnp.int32)))
    state = carry
    top, total, weighted = state
    attended = (
        (weighted / total[..., None]).transpose(1, 0, 2).reshape(-1, width).astype(jnp.bfloat16)
    )
    mixed = wide.reshape(-1, width) + jnp.dot(
        attended, o_weight, preferred_element_type=jnp.float32
    )
    return mixed.astype(jnp.bfloat16).reshape(rows, columns, levels, width)


def solution(mesh):
    placed = (P("lat", "lon", None, None), P(), P(), P(), P(), P(), P(), P())
    return jax.shard_map(
        body, mesh=mesh, in_specs=placed, out_specs=P("lat", "lon", None, None), check_vma=False
    )
```

profile of v0, /device:TPU:1, one launch (start us, length us, event | category | flops | bytes accessed | tf_op | source)
XLA Modules:
  0.0 453.6 jit_solution(10605950701415543880)
XLA Ops:
  33.7 134.1 %all-gather.2.cloned.1.call-done = bf16[2,10,256,2,1024]{4,2,3,1,0:T(8,128)(2,1)} async-done(((bf16[2,10,16,2,1024]{4,2,3,1,0:T(8,128)(2,1)}), bf16[2,10,256,2,1024]{4,2,3,1,0:T(8,128)(2,1)}) %all-gather.2.cloned.1.call-update) | async-done | bytes 20971536 | tf_op jit(solution)/shard_map/all_gather | solution.py:98
  167.8 38.5 %copy.30 = bf16[16,2,10,16,2,1024]{5,4,3,2,1,0:T(2,128)(2,1)} copy(bf16[16,2,10,16,2,1024]{5,3,0,4,2,1:T(8,128)(2,1)} %bitcast.33) | data formatting | bytes 41943040 | tf_op jit(solution)/shard_map/while | solution.py:106
  207.4 234.3 %while.16 = (s32[]{:T(128)}, f32[16,256]{1,0:T(8,128)S(1)}, f32[16,256]{1,0:T(8,128)S(1)}, f32[16,256,64]{1,2,0:T(8,128)}, s32[16]{0:T(128)S(1)}, /*index=5*/s32...) while((s32[]{:T(128)}, f32[16,256]{1,0:T(8,128)S(1)}, ...), condition=%wide.region_6.7_spmd, body=%wide.region_1.6_spmd.sunk | while | flops 346562560 | bytes 46137788 | solution.py:106
  209.8 12.3 %conditional.2 = ((f32[16,256]{1,0:T(8,128)S(1)}, f32[16,256]{1,0:T(8,128)S(1)}, f32[16,256,64]{1,2,0:T(8,128)})) conditional(s32[]{:T(128)} %convert_element_type.63, (f32[16,256]{1,0:T(8,128)S(1)}, f32[16,256]{1,0:T(8,128)S(1)}, f32[16,256,64]{1,2,0:T(8,128)}) %tuple.46, (bf16[16,2,10,16,2,1024]{5,4,3,2,1,0:T(2,128)(2,1)}, s32[]{:T(128)}, ...), branch_computations={%region_2.2_spmd, %region_3.5_spmd} | conditional | flops 346562560 | bytes 46137424 | solution.py:90
  217.1 4.9 %fusion.7 = f32[16,256,64]{1,2,0:T(8,128)} fusion(f32[16,320,256]{2,1,0:T(8,128)} %copy-done.2, f32[16,256]{1,0:T(8,128)S(1)} %max.3, bf16[320,16,64]{2,1,0:T(8,128)(2,1)S(1)} %squeeze.25, f32[16,256,64]{1,2,0:T(8,128)} %get-tuple-element.163, f32[16,256]{1,0:T(8,128)S(1)} %get-tuple-element.243), kind=kOutput, calls=%fused_computation.8 | convolution fusion | flops 172228608 | bytes 8028160 | tf_op jit(solution)/shard_map/while/body/eval_jaxpr/cond/branch_1_fun/hqk,khd->hqd/dot_general | solution.py:79
  224.4 12.3 %conditional.2 = ((f32[16,256]{1,0:T(8,128)S(1)}, f32[16,256]{1,0:T(8,128)S(1)}, f32[16,256,64]{1,2,0:T(8,128)})) conditional(s32[]{:T(128)} %convert_element_type.63, (f32[16,256]{1,0:T(8,128)S(1)}, f32[16,256]{1,0:T(8,128)S(1)}, f32[16,256,64]{1,2,0:T(8,128)}) %tuple.46, (bf16[16,2,10,16,2,1024]{5,4,3,2,1,0:T(2,128)(2,1)}, s32[]{:T(128)}, ...), branch_computations={%region_2.2_spmd, %region_3.5_spmd} | conditional | flops 346562560 | bytes 46137424 | solution.py:90
  239.1 12.3 %conditional.2 = ((f32[16,256]{1,0:T(8,128)S(1)}, f32[16,256]{1,0:T(8,128)S(1)}, f32[16,256,64]{1,2,0:T(8,128)})) conditional(s32[]{:T(128)} %convert_element_type.63, (f32[16,256]{1,0:T(8,128)S(1)}, f32[16,256]{1,0:T(8,128)S(1)}, f32[16,256,64]{1,2,0:T(8,128)}) %tuple.46, (bf16[16,2,10,16,2,1024]{5,4,3,2,1,0:T(2,128)(2,1)}, s32[]{:T(128)}, ...), branch_computations={%region_2.2_spmd, %region_3.5_spmd} | conditional | flops 346562560 | bytes 46137424 | solution.py:90
  246.4 4.9 %fusion.7 = f32[16,256,64]{1,2,0:T(8,128)} fusion(f32[16,320,256]{2,1,0:T(8,128)} %copy-done.2, f32[16,256]{1,0:T(8,128)S(1)} %max.3, bf16[320,16,64]{2,1,0:T(8,128)(2,1)S(1)} %squeeze.25, f32[16,256,64]{1,2,0:T(8,128)} %get-tuple-element.163, f32[16,256]{1,0:T(8,128)S(1)} %get-tuple-element.243), kind=kOutput, calls=%fused_computation.8 | convolution fusion | flops 172228608 | bytes 8028160 | tf_op jit(solution)/shard_map/while/body/eval_jaxpr/cond/branch_1_fun/hqk,khd->hqd/dot_general | solution.py:79
  253.7 12.3 %conditional.2 = ((f32[16,256]{1,0:T(8,128)S(1)}, f32[16,256]{1,0:T(8,128)S(1)}, f32[16,256,64]{1,2,0:T(8,128)})) conditional(s32[]{:T(128)} %convert_element_type.63, (f32[16,256]{1,0:T(8,128)S(1)}, f32[16,256]{1,0:T(8,128)S(1)}, f32[16,256,64]{1,2,0:T(8,128)}) %tuple.46, (bf16[16,2,10,16,2,1024]{5,4,3,2,1,0:T(2,128)(2,1)}, s32[]{:T(128)}, ...), branch_computations={%region_2.2_spmd, %region_3.5_spmd} | conditional | flops 346562560 | bytes 46137424 | solution.py:90
  268.4 12.3 %conditional.2 = ((f32[16,256]{1,0:T(8,128)S(1)}, f32[16,256]{1,0:T(8,128)S(1)}, f32[16,256,64]{1,2,0:T(8,128)})) conditional(s32[]{:T(128)} %convert_element_type.63, (f32[16,256]{1,0:T(8,128)S(1)}, f32[16,256]{1,0:T(8,128)S(1)}, f32[16,256,64]{1,2,0:T(8,128)}) %tuple.46, (bf16[16,2,10,16,2,1024]{5,4,3,2,1,0:T(2,128)(2,1)}, s32[]{:T(128)}, ...), branch_computations={%region_2.2_spmd, %region_3.5_spmd} | conditional | flops 346562560 | bytes 46137424 | solution.py:90
  275.7 4.9 %fusion.7 = f32[16,256,64]{1,2,0:T(8,128)} fusion(f32[16,320,256]{2,1,0:T(8,128)} %copy-done.2, f32[16,256]{1,0:T(8,128)S(1)} %max.3, bf16[320,16,64]{2,1,0:T(8,128)(2,1)S(1)} %squeeze.25, f32[16,256,64]{1,2,0:T(8,128)} %get-tuple-element.163, f32[16,256]{1,0:T(8,128)S(1)} %get-tuple-element.243), kind=kOutput, calls=%fused_computation.8 | convolution fusion | flops 172228608 | bytes 8028160 | tf_op jit(solution)/shard_map/while/body/eval_jaxpr/cond/branch_1_fun/hqk,khd->hqd/dot_general | solution.py:79
  283.0 12.3 %conditional.2 = ((f32[16,256]{1,0:T(8,128)S(1)}, f32[16,256]{1,0:T(8,128)S(1)}, f32[16,256,64]{1,2,0:T(8,128)})) conditional(s32[]{:T(128)} %convert_element_type.63, (f32[16,256]{1,0:T(8,128)S(1)}, f32[16,256]{1,0:T(8,128)S(1)}, f32[16,256,64]{1,2,0:T(8,128)}) %tuple.46, (bf16[16,2,10,16,2,1024]{5,4,3,2,1,0:T(2,128)(2,1)}, s32[]{:T(128)}, ...), branch_computations={%region_2.2_spmd, %region_3.5_spmd} | conditional | flops 346562560 | bytes 46137424 | solution.py:90
  297.6 12.3 %conditional.2 = ((f32[16,256]{1,0:T(8,128)S(1)}, f32[16,256]{1,0:T(8,128)S(1)}, f32[16,256,64]{1,2,0:T(8,128)})) conditional(s32[]{:T(128)} %convert_element_type.63, (f32[16,256]{1,0:T(8,128)S(1)}, f32[16,256]{1,0:T(8,128)S(1)}, f32[16,256,64]{1,2,0:T(8,128)}) %tuple.46, (bf16[16,2,10,16,2,1024]{5,4,3,2,1,0:T(2,128)(2,1)}, s32[]{:T(128)}, ...), branch_computations={%region_2.2_spmd, %region_3.5_spmd} | conditional | flops 346562560 | bytes 46137424 | solution.py:90
  305.0 4.9 %fusion.7 = f32[16,256,64]{1,2,0:T(8,128)} fusion(f32[16,320,256]{2,1,0:T(8,128)} %copy-done.2, f32[16,256]{1,0:T(8,128)S(1)} %max.3, bf16[320,16,64]{2,1,0:T(8,128)(2,1)S(1)} %squeeze.25, f32[16,256,64]{1,2,0:T(8,128)} %get-tuple-element.163, f32[16,256]{1,0:T(8,128)S(1)} %get-tuple-element.243), kind=kOutput, calls=%fused_computation.8 | convolution fusion | flops 172228608 | bytes 8028160 | tf_op jit(solution)/shard_map/while/body/eval_jaxpr/cond/branch_1_fun/hqk,khd->hqd/dot_general | solution.py:79
  312.3 12.3 %conditional.2 = ((f32[16,256]{1,0:T(8,128)S(1)}, f32[16,256]{1,0:T(8,128)S(1)}, f32[16,256,64]{1,2,0:T(8,128)})) conditional(s32[]{:T(128)} %convert_element_type.63, (f32[16,256]{1,0:T(8,128)S(1)}, f32[16,256]{1,0:T(8,128)S(1)}, f32[16,256,64]{1,2,0:T(8,128)}) %tuple.46, (bf16[16,2,10,16,2,1024]{5,4,3,2,1,0:T(2,128)(2,1)}, s32[]{:T(128)}, ...), branch_computations={%region_2.2_spmd, %region_3.5_spmd} | conditional | flops 346562560 | bytes 46137424 | solution.py:90
  326.9 12.3 %conditional.2 = ((f32[16,256]{1,0:T(8,128)S(1)}, f32[16,256]{1,0:T(8,128)S(1)}, f32[16,256,64]{1,2,0:T(8,128)})) conditional(s32[]{:T(128)} %convert_element_type.63, (f32[16,256]{1,0:T(8,128)S(1)}, f32[16,256]{1,0:T(8,128)S(1)}, f32[16,256,64]{1,2,0:T(8,128)}) %tuple.46, (bf16[16,2,10,16,2,1024]{5,4,3,2,1,0:T(2,128)(2,1)}, s32[]{:T(128)}, ...), branch_computations={%region_2.2_spmd, %region_3.5_spmd} | conditional | flops 346562560 | bytes 46137424 | solution.py:90
  334.3 4.9 %fusion.7 = f32[16,256,64]{1,2,0:T(8,128)} fusion(f32[16,320,256]{2,1,0:T(8,128)} %copy-done.2, f32[16,256]{1,0:T(8,128)S(1)} %max.3, bf16[320,16,64]{2,1,0:T(8,128)(2,1)S(1)} %squeeze.25, f32[16,256,64]{1,2,0:T(8,128)} %get-tuple-element.163, f32[16,256]{1,0:T(8,128)S(1)} %get-tuple-element.243), kind=kOutput, calls=%fused_computation.8 | convolution fusion | flops 172228608 | bytes 8028160 | tf_op jit(solution)/shard_map/while/body/eval_jaxpr/cond/branch_1_fun/hqk,khd->hqd/dot_general | solution.py:79
  341.6 12.3 %conditional.2 = ((f32[16,256]{1,0:T(8,128)S(1)}, f32[16,256]{1,0:T(8,128)S(1)}, f32[16,256,64]{1,2,0:T(8,128)})) conditional(s32[]{:T(128)} %convert_element_type.63, (f32[16,256]{1,0:T(8,128)S(1)}, f32[16,256]{1,0:T(8,128)S(1)}, f32[16,256,64]{1,2,0:T(8,128)}) %tuple.46, (bf16[16,2,10,16,2,1024]{5,4,3,2,1,0:T(2,128)(2,1)}, s32[]{:T(128)}, ...), branch_computations={%region_2.2_spmd, %region_3.5_spmd} | conditional | flops 346562560 | bytes 46137424 | solution.py:90
  356.2 12.3 %conditional.2 = ((f32[16,256]{1,0:T(8,128)S(1)}, f32[16,256]{1,0:T(8,128)S(1)}, f32[16,256,64]{1,2,0:T(8,128)})) conditional(s32[]{:T(128)} %convert_element_type.63, (f32[16,256]{1,0:T(8,128)S(1)}, f32[16,256]{1,0:T(8,128)S(1)}, f32[16,256,64]{1,2,0:T(8,128)}) %tuple.46, (bf16[16,2,10,16,2,1024]{5,4,3,2,1,0:T(2,128)(2,1)}, s32[]{:T(128)}, ...), branch_computations={%region_2.2_spmd, %region_3.5_spmd} | conditional | flops 346562560 | bytes 46137424 | solution.py:90
  370.9 12.3 %conditional.2 = ((f32[16,256]{1,0:T(8,128)S(1)}, f32[16,256]{1,0:T(8,128)S(1)}, f32[16,256,64]{1,2,0:T(8,128)})) conditional(s32[]{:T(128)} %convert_element_type.63, (f32[16,256]{1,0:T(8,128)S(1)}, f32[16,256]{1,0:T(8,128)S(1)}, f32[16,256,64]{1,2,0:T(8,128)}) %tuple.46, (bf16[16,2,10,16,2,1024]{5,4,3,2,1,0:T(2,128)(2,1)}, s32[]{:T(128)}, ...), branch_computations={%region_2.2_spmd, %region_3.5_spmd} | conditional | flops 346562560 | bytes 46137424 | solution.py:90
  385.5 12.3 %conditional.2 = ((f32[16,256]{1,0:T(8,128)S(1)}, f32[16,256]{1,0:T(8,128)S(1)}, f32[16,256,64]{1,2,0:T(8,128)})) conditional(s32[]{:T(128)} %convert_element_type.63, (f32[16,256]{1,0:T(8,128)S(1)}, f32[16,256]{1,0:T(8,128)S(1)}, f32[16,256,64]{1,2,0:T(8,128)}) %tuple.46, (bf16[16,2,10,16,2,1024]{5,4,3,2,1,0:T(2,128)(2,1)}, s32[]{:T(128)}, ...), branch_computations={%region_2.2_spmd, %region_3.5_spmd} | conditional | flops 346562560 | bytes 46137424 | solution.py:90
  400.2 12.3 %conditional.2 = ((f32[16,256]{1,0:T(8,128)S(1)}, f32[16,256]{1,0:T(8,128)S(1)}, f32[16,256,64]{1,2,0:T(8,128)})) conditional(s32[]{:T(128)} %convert_element_type.63, (f32[16,256]{1,0:T(8,128)S(1)}, f32[16,256]{1,0:T(8,128)S(1)}, f32[16,256,64]{1,2,0:T(8,128)}) %tuple.46, (bf16[16,2,10,16,2,1024]{5,4,3,2,1,0:T(2,128)(2,1)}, s32[]{:T(128)}, ...), branch_computations={%region_2.2_spmd, %region_3.5_spmd} | conditional | flops 346562560 | bytes 46137424 | solution.py:90
  414.8 12.3 %conditional.2 = ((f32[16,256]{1,0:T(8,128)S(1)}, f32[16,256]{1,0:T(8,128)S(1)}, f32[16,256,64]{1,2,0:T(8,128)})) conditional(s32[]{:T(128)} %convert_element_type.63, (f32[16,256]{1,0:T(8,128)S(1)}, f32[16,256]{1,0:T(8,128)S(1)}, f32[16,256,64]{1,2,0:T(8,128)}) %tuple.46, (bf16[16,2,10,16,2,1024]{5,4,3,2,1,0:T(2,128)(2,1)}, s32[]{:T(128)}, ...), branch_computations={%region_2.2_spmd, %region_3.5_spmd} | conditional | flops 346562560 | bytes 46137424 | solution.py:90
  429.4 12.3 %conditional.2 = ((f32[16,256]{1,0:T(8,128)S(1)}, f32[16,256]{1,0:T(8,128)S(1)}, f32[16,256,64]{1,2,0:T(8,128)})) conditional(s32[]{:T(128)} %convert_element_type.63, (f32[16,256]{1,0:T(8,128)S(1)}, f32[16,256]{1,0:T(8,128)S(1)}, f32[16,256,64]{1,2,0:T(8,128)}) %tuple.46, (bf16[16,2,10,16,2,1024]{5,4,3,2,1,0:T(2,128)(2,1)}, s32[]{:T(128)}, ...), branch_computations={%region_2.2_spmd, %region_3.5_spmd} | conditional | flops 346562560 | bytes 46137424 | solution.py:90
  (236 shorter events, 212.8 us)
Async XLA Ops:
  6.5 4.6 %copy-start = (bf16[1024,1024]{1,0:T(8,128)(2,1)S(1)}, bf16[1024,1024]{1,0:T(8,128)(2,1)}, u32[]{:S(2)}) copy-start(bf16[1024,1024]{1,0:T(8,128)(2,1)} %param.15) | copy-start | bytes 6291460
  6.5 161.3 %all-gather.2.cloned.1.call-start = ((), (), s32[]{:S(2)}) async-start(), calls=%async_computation | async-start | bytes 22282240 | tf_op jit(solution)/shard_map/all_gather | solution.py:98
  14.9 12.6 %collective-permute-start = (bf16[2,2,16,2,1024]{4,2,3,1,0:T(8,128)(2,1)S(1)}, bf16[2,2,16,2,1024]{4,2,3,1,0:T(8,128)(2,1)S(1)}, u32[]{:S(2)}, u32[]{:S(2)}) collective-permute-start(bf16[2,2,16,2,1024]{4,2,3,1,0:T(8,128)(2,1)S(1)} %pad_maximum_fusion.1), channel_id=1, source_target_pairs={{0,8},{1,9},{2,10},{3,11},{4,12},{5,13},{6,14},{7,15},{8,0},{9,1},... | collective-permute-start | bytes 786440 | tf_op jit(solution)/shard_map/ppermute | solution.py:25
  18.6 7.8 %collective-permute-start.1 = (bf16[2,1,16,2,1024]{4,2,3,1,0:T(8,128)(2,1)S(1)}, bf16[2,1,16,2,1024]{4,2,3,1,0:T(8,128)(2,1)S(1)}, u32[]{:S(2)}, u32[]{:S(2)}) collective-permute-start(bf16[2,1,16,2,1024]{4,2,3,1,0:T(8,128)(2,1)S(1)} %get-tuple-element.248), channel_id=1, source_target_pairs={{0,16},{16,32},{32,48},{48,64},{64,80},{80,96},{96,112},{112,128},... | collective-permute-start | bytes 393224 | tf_op jit(solution)/shard_map/ppermute | solution.py:16
  20.8 6.8 %collective-permute-start.2 = (bf16[2,1,16,2,1024]{4,2,3,1,0:T(8,128)(2,1)S(1)}, bf16[2,1,16,2,1024]{4,2,3,1,0:T(8,128)(2,1)S(1)}, u32[]{:S(2)}, u32[]{:S(2)}) collective-permute-start(bf16[2,1,16,2,1024]{4,2,3,1,0:T(8,128)(2,1)S(1)} %get-tuple-element.249), channel_id=1, source_target_pairs={{16,0},{32,16},{48,32},{64,48},{80,64},{96,80},{112,96},{128,112},... | collective-permute-start | bytes 393224 | tf_op jit(solution)/shard_map/ppermute | solution.py:17
  28.8 1.8 copy-start.6
  214.0 2.3 copy-start.2
  228.7 2.3 copy-start.2
  243.3 2.3 copy-start.2
  258.0 2.3 copy-start.2
  272.6 2.3 copy-start.2
  287.2 2.3 copy-start.2
  301.9 2.3 copy-start.2
  316.5 2.3 copy-start.2
  331.2 2.3 copy-start.2
  345.8 2.3 copy-start.2
  360.5 2.3 copy-start.2
  375.1 2.3 copy-start.2
  389.8 2.3 copy-start.2
  404.4 2.3 copy-start.2
  419.0 2.3 copy-start.2
  433.7 2.3 copy-start.2
  441.7 1.5 copy-start.4
  443.2 3.6 copy-start.1
  (2 other events, 2.5 us)
Sparse Core Ops, SparseCore 0:
  29.0 138.8 all-gather.1
where the time goes:
time: 455 us; the launch traced here: 454 us
  local copies, waits for them, and re-layouts  142 us (31%)
  waiting for transfers between devices  139 us (31%)
  matrix products  99.8 us (22%)
  loops' own time  30 us (7%)
  other arithmetic  21.2 us (5%)
  between operations  13.6 us (3%)
  starting transfers between devices  7.33 us (2%)
    all_gather x1, waiting for transfers between devices, body(): piece = lax.all_gather(extended, 'lon', axis=2, tiled=True)  134 us
    dot_general x16, matrix products, update(): jnp.einsum('hqk,khd->hqd', raw.astype(jnp.bfloat16), value_heads, preferr...  78.7 us
    slice x16, local copies, waits for them, and re-layouts, update(): value_heads = piece[1].reshape(-1, heads, HD)  41.9 us
    while x1, local copies, waits for them, and re-layouts, body(): lax.scan(advance, carry, (split, jnp.arange(count, dtype=jnp.int32)))  38.5 us
    another operation x1, loops' own time, body(): lax.scan(advance, carry, (split, jnp.arange(count, dtype=jnp.int32)))  28.8 us
    cond x48, local copies, waits for them, and re-layouts  23.1 us
    reduce_sum x16, other arithmetic, update(): total = total * fade + jnp.sum(raw, -1)  14.1 us
    dot_general x16, matrix products, update(): jnp.einsum('qhd,khd->hqk', query_heads, key_heads, preferred_element_type...  13.4 us
  transfers between devices with their start and end apart: 4, of which 3 were waited for; matrix products, arithmetic and copies ran while one was open for 1% of the time, Pallas kernels for 0%

commit v1 on v0

--- a/solution.py
+++ b/solution.py
@@ -95,7 +95,9 @@
         jnp.zeros((heads, count_queries, HD), jnp.float32),
     )
     carry = initial
-    piece = lax.all_gather(extended, "lon", axis=2, tiled=True)
+    piece = jnp.concatenate(
+        lax.all_to_all(jnp.stack([extended] * lax.axis_size("lon")), "lon", 0, 0), axis=2
+    )
     count = piece.shape[2] // columns
     split = jnp.moveaxis(piece.reshape(2, rows + 2, count, columns, levels, width), 2, 0)
 

time: 455 us -> 623 us (1.37); the launches traced: 454 us -> 613 us
  waiting for transfers between devices: 139 us -> 320 us
  local copies, waits for them, and re-layouts: 142 us -> 124 us
  between operations: 13.6 us -> 0.17 us
  starting transfers between devices: 7.33 us -> 15.6 us
    all_to_all x0 -> x1, waiting for transfers between devices: none -> 314 us  [body(): lax.all_to_all(jnp.stack([extended] * lax.axis_size('lon')), 'lon', 0, 0)]
    all_gather x1 -> x0, waiting for transfers between devices: 134 us -> none  [body(): piece = lax.all_gather(extended, 'lon', axis=2, tiled=True)]
    while x1 -> x0, local copies, waits for them, and re-layouts: 38.5 us -> none  [body(): lax.scan(advance, carry, (split, jnp.arange(count, dtype=jnp.int32)))]
    another operation x0 -> x1, local copies, waits for them, and re-layouts: none -> 17.9 us  [body(): jnp.stack([extended] * lax.axis_size('lon'))]
    all_to_all x0 -> x1, starting transfers between devices: none -> 8.42 us  [body(): lax.all_to_all(jnp.stack([extended] * lax.axis_size('lon')), 'lon', 0, 0)]
where the time goes in v1:
time: 623 us; the launch traced here: 613 us
  waiting for transfers between devices  320 us (51%)
  local copies, waits for them, and re-layouts  124 us (20%)
  matrix products  99.9 us (16%)
  loops' own time  31.1 us (5%)
  other arithmetic  22.6 us (4%)
  starting transfers between devices  15.6 us (3%)
    all_to_all x1, waiting for transfers between devices, body(): lax.all_to_all(jnp.stack([extended] * lax.axis_size('lon')), 'lon', 0, 0)  314 us
    dot_general x16, matrix products, update(): jnp.einsum('hqk,khd->hqd', raw.astype(jnp.bfloat16), value_heads, preferr...  78.8 us
    slice x16, local copies, waits for them, and re-layouts, update(): value_heads = piece[1].reshape(-1, heads, HD)  41.9 us
    another operation x1, loops' own time, body(): lax.scan(advance, carry, (split, jnp.arange(count, dtype=jnp.int32)))  29.9 us
    cond x48, local copies, waits for them, and re-layouts  22.9 us
    another operation x1, local copies, waits for them, and re-layouts, body(): jnp.stack([extended] * lax.axis_size('lon'))  17.9 us
    reduce_sum x16, other arithmetic, update(): total = total * fade + jnp.sum(raw, -1)  14.1 us
    dot_general x16, matrix products, update(): jnp.einsum('qhd,khd->hqk', query_heads, key_heads, preferred_element_type...  13.4 us
  transfers between devices with their start and end apart: 4, of which 3 were waited for; matrix products, arithmetic and copies ran while one was open for 1% of the time, Pallas kernels for 0%

profile of v1, /device:TPU:1, one launch (start us, length us, event | category | flops | bytes accessed | tf_op | source)
XLA Modules:
  0.0 612.7 jit_solution(11068890220083350508)
XLA Ops:
  24.3 17.9 %stack.8 = bf16[16,2,10,16,2,1024]{5,4,3,2,1,0:T(2,128)(2,1)} broadcast(bf16[2,10,16,2,1024]{4,3,2,1,0:T(2,128)(2,1)S(1)} %pad_maximum_fusion), dimensions={1,2,3,4,5} | broadcast | bytes 22282240 | tf_op jit(solution)/shard_map/stack | solution.py:99
  42.3 8.4 %all-to-all-start = ((bf16[16,2,10,16,2,1024]{5,4,3,2,1,0:T(2,128)(2,1)}), bf16[16,2,10,16,2,1024]{5,4,3,2,1,0:T(2,128)(2,1)}, u32[]{:S(2)}, u32[]{:S(2)}) async-start(bf16[16,2,10,16,2,1024]{5,4,3,2,1,0:T(2,128)(2,1)} %stack.8), calls=%async_computation | async-start | bytes 41943040 | tf_op jit(solution)/shard_map/all_to_all | solution.py:99
  55.6 314.3 %all-to-all-done = bf16[16,2,10,16,2,1024]{5,4,3,2,1,0:T(2,128)(2,1)} async-done(((bf16[16,2,10,16,2,1024]{5,4,3,2,1,0:T(2,128)(2,1)}), bf16[16,2,10,16,2,1024]{5,4,3,2,1,0:T(2,128)(2,1)}, u32[]{:S(2)}, u32[]{:S(2)}) %all-to-all-start) | async-done | bytes 20971552 | tf_op jit(solution)/shard_map/all_to_all | solution.py:99
  370.9 236.8 %while.16 = (s32[]{:T(128)}, f32[16,256]{1,0:T(8,128)S(1)}, f32[16,256]{1,0:T(8,128)S(1)}, f32[16,256,64]{1,2,0:T(8,128)}, s32[16]{0:T(128)S(1)}, /*index=5*/s32...) while((s32[]{:T(128)}, f32[16,256]{1,0:T(8,128)S(1)}, ...), condition=%wide.region_6.7_spmd, body=%wide.region_1.6_spmd.sunk | while | flops 346562560 | bytes 46137788 | solution.py:108
  373.5 12.3 %conditional.2 = ((f32[16,256]{1,0:T(8,128)S(1)}, f32[16,256]{1,0:T(8,128)S(1)}, f32[16,256,64]{1,2,0:T(8,128)})) conditional(s32[]{:T(128)} %convert_element_type.63, (f32[16,256]{1,0:T(8,128)S(1)}, f32[16,256]{1,0:T(8,128)S(1)}, f32[16,256,64]{1,2,0:T(8,128)}) %tuple.43, (bf16[16,2,10,16,2,1024]{5,4,3,2,1,0:T(2,128)(2,1)}, s32[]{:T(128)}, ...), branch_computations={%region_2.2_spmd, %region_3.5_spmd} | conditional | flops 346562560 | bytes 46137424 | solution.py:90
  380.8 4.9 fusion.7
  388.3 12.3 %conditional.2 = ((f32[16,256]{1,0:T(8,128)S(1)}, f32[16,256]{1,0:T(8,128)S(1)}, f32[16,256,64]{1,2,0:T(8,128)})) conditional(s32[]{:T(128)} %convert_element_type.63, (f32[16,256]{1,0:T(8,128)S(1)}, f32[16,256]{1,0:T(8,128)S(1)}, f32[16,256,64]{1,2,0:T(8,128)}) %tuple.43, (bf16[16,2,10,16,2,1024]{5,4,3,2,1,0:T(2,128)(2,1)}, s32[]{:T(128)}, ...), branch_computations={%region_2.2_spmd, %region_3.5_spmd} | conditional | flops 346562560 | bytes 46137424 | solution.py:90
  403.1 12.3 %conditional.2 = ((f32[16,256]{1,0:T(8,128)S(1)}, f32[16,256]{1,0:T(8,128)S(1)}, f32[16,256,64]{1,2,0:T(8,128)})) conditional(s32[]{:T(128)} %convert_element_type.63, (f32[16,256]{1,0:T(8,128)S(1)}, f32[16,256]{1,0:T(8,128)S(1)}, f32[16,256,64]{1,2,0:T(8,128)}) %tuple.43, (bf16[16,2,10,16,2,1024]{5,4,3,2,1,0:T(2,128)(2,1)}, s32[]{:T(128)}, ...), branch_computations={%region_2.2_spmd, %region_3.5_spmd} | conditional | flops 346562560 | bytes 46137424 | solution.py:90
  410.4 4.9 fusion.7
  417.9 12.3 %conditional.2 = ((f32[16,256]{1,0:T(8,128)S(1)}, f32[16,256]{1,0:T(8,128)S(1)}, f32[16,256,64]{1,2,0:T(8,128)})) conditional(s32[]{:T(128)} %convert_element_type.63, (f32[16,256]{1,0:T(8,128)S(1)}, f32[16,256]{1,0:T(8,128)S(1)}, f32[16,256,64]{1,2,0:T(8,128)}) %tuple.43, (bf16[16,2,10,16,2,1024]{5,4,3,2,1,0:T(2,128)(2,1)}, s32[]{:T(128)}, ...), branch_computations={%region_2.2_spmd, %region_3.5_spmd} | conditional | flops 346562560 | bytes 46137424 | solution.py:90
  432.7 12.3 %conditional.2 = ((f32[16,256]{1,0:T(8,128)S(1)}, f32[16,256]{1,0:T(8,128)S(1)}, f32[16,256,64]{1,2,0:T(8,128)})) conditional(s32[]{:T(128)} %convert_element_type.63, (f32[16,256]{1,0:T(8,128)S(1)}, f32[16,256]{1,0:T(8,128)S(1)}, f32[16,256,64]{1,2,0:T(8,128)}) %tuple.43, (bf16[16,2,10,16,2,1024]{5,4,3,2,1,0:T(2,128)(2,1)}, s32[]{:T(128)}, ...), branch_computations={%region_2.2_spmd, %region_3.5_spmd} | conditional | flops 346562560 | bytes 46137424 | solution.py:90
  440.0 4.9 fusion.7
  447.5 12.3 %conditional.2 = ((f32[16,256]{1,0:T(8,128)S(1)}, f32[16,256]{1,0:T(8,128)S(1)}, f32[16,256,64]{1,2,0:T(8,128)})) conditional(s32[]{:T(128)} %convert_element_type.63, (f32[16,256]{1,0:T(8,128)S(1)}, f32[16,256]{1,0:T(8,128)S(1)}, f32[16,256,64]{1,2,0:T(8,128)}) %tuple.43, (bf16[16,2,10,16,2,1024]{5,4,3,2,1,0:T(2,128)(2,1)}, s32[]{:T(128)}, ...), branch_computations={%region_2.2_spmd, %region_3.5_spmd} | conditional | flops 346562560 | bytes 46137424 | solution.py:90
  462.3 12.3 %conditional.2 = ((f32[16,256]{1,0:T(8,128)S(1)}, f32[16,256]{1,0:T(8,128)S(1)}, f32[16,256,64]{1,2,0:T(8,128)})) conditional(s32[]{:T(128)} %convert_element_type.63, (f32[16,256]{1,0:T(8,128)S(1)}, f32[16,256]{1,0:T(8,128)S(1)}, f32[16,256,64]{1,2,0:T(8,128)}) %tuple.43, (bf16[16,2,10,16,2,1024]{5,4,3,2,1,0:T(2,128)(2,1)}, s32[]{:T(128)}, ...), branch_computations={%region_2.2_spmd, %region_3.5_spmd} | conditional | flops 346562560 | bytes 46137424 | solution.py:90
  469.6 4.9 fusion.7
  477.1 12.3 %conditional.2 = ((f32[16,256]{1,0:T(8,128)S(1)}, f32[16,256]{1,0:T(8,128)S(1)}, f32[16,256,64]{1,2,0:T(8,128)})) conditional(s32[]{:T(128)} %convert_element_type.63, (f32[16,256]{1,0:T(8,128)S(1)}, f32[16,256]{1,0:T(8,128)S(1)}, f32[16,256,64]{1,2,0:T(8,128)}) %tuple.43, (bf16[16,2,10,16,2,1024]{5,4,3,2,1,0:T(2,128)(2,1)}, s32[]{:T(128)}, ...), branch_computations={%region_2.2_spmd, %region_3.5_spmd} | conditional | flops 346562560 | bytes 46137424 | solution.py:90
  491.9 12.3 %conditional.2 = ((f32[16,256]{1,0:T(8,128)S(1)}, f32[16,256]{1,0:T(8,128)S(1)}, f32[16,256,64]{1,2,0:T(8,128)})) conditional(s32[]{:T(128)} %convert_element_type.63, (f32[16,256]{1,0:T(8,128)S(1)}, f32[16,256]{1,0:T(8,128)S(1)}, f32[16,256,64]{1,2,0:T(8,128)}) %tuple.43, (bf16[16,2,10,16,2,1024]{5,4,3,2,1,0:T(2,128)(2,1)}, s32[]{:T(128)}, ...), branch_computations={%region_2.2_spmd, %region_3.5_spmd} | conditional | flops 346562560 | bytes 46137424 | solution.py:90
  506.7 12.3 %conditional.2 = ((f32[16,256]{1,0:T(8,128)S(1)}, f32[16,256]{1,0:T(8,128)S(1)}, f32[16,256,64]{1,2,0:T(8,128)})) conditional(s32[]{:T(128)} %convert_element_type.63, (f32[16,256]{1,0:T(8,128)S(1)}, f32[16,256]{1,0:T(8,128)S(1)}, f32[16,256,64]{1,2,0:T(8,128)}) %tuple.43, (bf16[16,2,10,16,2,1024]{5,4,3,2,1,0:T(2,128)(2,1)}, s32[]{:T(128)}, ...), branch_computations={%region_2.2_spmd, %region_3.5_spmd} | conditional | flops 346562560 | bytes 46137424 | solution.py:90
  521.5 12.3 %conditional.2 = ((f32[16,256]{1,0:T(8,128)S(1)}, f32[16,256]{1,0:T(8,128)S(1)}, f32[16,256,64]{1,2,0:T(8,128)})) conditional(s32[]{:T(128)} %convert_element_type.63, (f32[16,256]{1,0:T(8,128)S(1)}, f32[16,256]{1,0:T(8,128)S(1)}, f32[16,256,64]{1,2,0:T(8,128)}) %tuple.43, (bf16[16,2,10,16,2,1024]{5,4,3,2,1,0:T(2,128)(2,1)}, s32[]{:T(128)}, ...), branch_computations={%region_2.2_spmd, %region_3.5_spmd} | conditional | flops 346562560 | bytes 46137424 | solution.py:90
  536.3 12.3 %conditional.2 = ((f32[16,256]{1,0:T(8,128)S(1)}, f32[16,256]{1,0:T(8,128)S(1)}, f32[16,256,64]{1,2,0:T(8,128)})) conditional(s32[]{:T(128)} %convert_element_type.63, (f32[16,256]{1,0:T(8,128)S(1)}, f32[16,256]{1,0:T(8,128)S(1)}, f32[16,256,64]{1,2,0:T(8,128)}) %tuple.43, (bf16[16,2,10,16,2,1024]{5,4,3,2,1,0:T(2,128)(2,1)}, s32[]{:T(128)}, ...), branch_computations={%region_2.2_spmd, %region_3.5_spmd} | conditional | flops 346562560 | bytes 46137424 | solution.py:90
  551.1 12.3 %conditional.2 = ((f32[16,256]{1,0:T(8,128)S(1)}, f32[16,256]{1,0:T(8,128)S(1)}, f32[16,256,64]{1,2,0:T(8,128)})) conditional(s32[]{:T(128)} %convert_element_type.63, (f32[16,256]{1,0:T(8,128)S(1)}, f32[16,256]{1,0:T(8,128)S(1)}, f32[16,256,64]{1,2,0:T(8,128)}) %tuple.43, (bf16[16,2,10,16,2,1024]{5,4,3,2,1,0:T(2,128)(2,1)}, s32[]{:T(128)}, ...), branch_computations={%region_2.2_spmd, %region_3.5_spmd} | conditional | flops 346562560 | bytes 46137424 | solution.py:90
  565.9 12.3 %conditional.2 = ((f32[16,256]{1,0:T(8,128)S(1)}, f32[16,256]{1,0:T(8,128)S(1)}, f32[16,256,64]{1,2,0:T(8,128)})) conditional(s32[]{:T(128)} %convert_element_type.63, (f32[16,256]{1,0:T(8,128)S(1)}, f32[16,256]{1,0:T(8,128)S(1)}, f32[16,256,64]{1,2,0:T(8,128)}) %tuple.43, (bf16[16,2,10,16,2,1024]{5,4,3,2,1,0:T(2,128)(2,1)}, s32[]{:T(128)}, ...), branch_computations={%region_2.2_spmd, %region_3.5_spmd} | conditional | flops 346562560 | bytes 46137424 | solution.py:90
  580.7 12.3 %conditional.2 = ((f32[16,256]{1,0:T(8,128)S(1)}, f32[16,256]{1,0:T(8,128)S(1)}, f32[16,256,64]{1,2,0:T(8,128)})) conditional(s32[]{:T(128)} %convert_element_type.63, (f32[16,256]{1,0:T(8,128)S(1)}, f32[16,256]{1,0:T(8,128)S(1)}, f32[16,256,64]{1,2,0:T(8,128)}) %tuple.43, (bf16[16,2,10,16,2,1024]{5,4,3,2,1,0:T(2,128)(2,1)}, s32[]{:T(128)}, ...), branch_computations={%region_2.2_spmd, %region_3.5_spmd} | conditional | flops 346562560 | bytes 46137424 | solution.py:90
  595.5 12.3 %conditional.2 = ((f32[16,256]{1,0:T(8,128)S(1)}, f32[16,256]{1,0:T(8,128)S(1)}, f32[16,256,64]{1,2,0:T(8,128)})) conditional(s32[]{:T(128)} %convert_element_type.63, (f32[16,256]{1,0:T(8,128)S(1)}, f32[16,256]{1,0:T(8,128)S(1)}, f32[16,256,64]{1,2,0:T(8,128)}) %tuple.43, (bf16[16,2,10,16,2,1024]{5,4,3,2,1,0:T(2,128)(2,1)}, s32[]{:T(128)}, ...), branch_computations={%region_2.2_spmd, %region_3.5_spmd} | conditional | flops 346562560 | bytes 46137424 | solution.py:90
  (235 shorter events, 221.1 us)
Async XLA Ops:
  0.0 4.6 copy-start
  9.4 12.6 %collective-permute-start = (bf16[2,2,16,2,1024]{4,3,2,1,0:T(2,128)(2,1)S(1)}, bf16[2,2,16,2,1024]{4,3,2,1,0:T(2,128)(2,1)S(1)}, u32[]{:S(2)}, u32[]{:S(2)}) collective-permute-start(bf16[2,2,16,2,1024]{4,3,2,1,0:T(2,128)(2,1)S(1)} %pad_maximum_fusion.1), channel_id=1, source_target_pairs={{0,8},{1,9},{2,10},{3,11},{4,12},{5,13},{6,14},{7,15},{8,0},{9,1},... | collective-permute-start | bytes 786440 | tf_op jit(solution)/shard_map/ppermute | solution.py:25
  13.0 7.8 %collective-permute-start.1 = (bf16[2,1,16,2,1024]{4,3,2,1,0:T(2,128)(2,1)S(1)}, bf16[2,1,16,2,1024]{4,3,2,1,0:T(2,128)(2,1)S(1)}, u32[]{:S(2)}, u32[]{:S(2)}) collective-permute-start(bf16[2,1,16,2,1024]{4,3,2,1,0:T(2,128)(2,1)S(1)} %get-tuple-element.218), channel_id=1, source_target_pairs={{0,16},{16,32},{32,48},{48,64},{64,80},{80,96},{96,112},{112,128},... | collective-permute-start | bytes 393224 | tf_op jit(solution)/shard_map/ppermute | solution.py:16
  15.3 6.8 %collective-permute-start.2 = (bf16[2,1,16,2,1024]{4,3,2,1,0:T(2,128)(2,1)S(1)}, bf16[2,1,16,2,1024]{4,3,2,1,0:T(2,128)(2,1)S(1)}, u32[]{:S(2)}, u32[]{:S(2)}) collective-permute-start(bf16[2,1,16,2,1024]{4,3,2,1,0:T(2,128)(2,1)S(1)} %get-tuple-element.219), channel_id=1, source_target_pairs={{16,0},{32,16},{48,32},{64,48},{80,64},{96,80},{112,96},{128,112},... | collective-permute-start | bytes 393224 | tf_op jit(solution)/shard_map/ppermute | solution.py:17
  42.3 8.4 %copy-start.3 = (bf16[8,16,2,1024]{3,2,1,0:T(2,128)(2,1)S(1)}, bf16[8,16,2,1024]{3,2,1,0:T(2,128)(2,1)}, u32[]{:S(2)}) copy-start(bf16[8,16,2,1024]{3,2,1,0:T(2,128)(2,1)} %param.12) | copy-start | bytes 1572868
  42.3 9.6 %copy-start.5 = (s32[16]{0:T(128)S(1)}, s32[16]{0:T(128)}, u32[]{:S(2)}) copy-start(s32[16]{0:T(128)} %param.18) | copy-start | bytes 196
  42.3 10.2 %copy-start.6 = (s32[16]{0:T(128)S(1)}, s32[16]{0:T(128)}, u32[]{:S(2)}) copy-start(s32[16]{0:T(128)} %param.19) | copy-start | bytes 196
  42.3 327.6 %all-to-all-start = ((bf16[16,2,10,16,2,1024]{5,4,3,2,1,0:T(2,128)(2,1)}), bf16[16,2,10,16,2,1024]{5,4,3,2,1,0:T(2,128)(2,1)}, u32[]{:S(2)}, u32[]{:S(2)}) async-start(bf16[16,2,10,16,2,1024]{5,4,3,2,1,0:T(2,128)(2,1)} %stack.8), calls=%async_computation | async-start | bytes 41943040 | tf_op jit(solution)/shard_map/all_to_all | solution.py:99
  377.7 2.3 copy-start.2
  392.5 2.3 copy-start.2
  407.3 2.3 copy-start.2
  422.1 2.3 copy-start.2
  436.9 2.3 copy-start.2
  451.7 2.3 copy-start.2
  466.5 2.3 copy-start.2
  481.3 2.3 copy-start.2
  496.1 2.3 copy-start.2
  510.9 2.3 copy-start.2
  525.7 2.3 copy-start.2
  540.5 2.3 copy-start.2
  555.3 2.3 copy-start.2
  570.1 2.3 copy-start.2
  584.9 2.3 copy-start.2
  609.2 3.6 copy-start.1
  (2 other events, 3.9 us)
